TPU v7x, 32 devices: a whole 2x2x4 slice. The times are simulated.
32 devices in a mesh: parts: 2 (over y), users: 16 (over z, x, core).
Axes of the slice: x: 2, y: 2, z: 4, core: 2. Of those that a mesh axis runs over, the one named last changes fastest.
Arguments:
- candidates: bfloat16 [512, 512], P(('parts', 'users')), parts along dimension 0, may hold values from -6 to 6
- candidate_user: int32 [512], P(('parts', 'users')), parts along dimension 0, may hold values from 0 to 7
- events: bfloat16 [65536, 512], P(('parts', 'users')), parts along dimension 0, may hold values from -6 to 6
- event_user: int32 [65536], P(('parts', 'users')), parts along dimension 0, may hold values from 0 to 7, never falling along the last dimension, each value on 1 to 12288 neighbouring positions
- event_mask: int32 [65536], P(('parts', 'users')), parts along dimension 0, may hold values 0 or 1
- query_weight: bfloat16 [512, 512], replicated, may hold values from -0.25 to 0.25
- key_weight: bfloat16 [512, 512], replicated, may hold values from -0.25 to 0.25
- value_weight: bfloat16 [512, 512], replicated, may hold values from -2 to 2
- gate_weight: bfloat16 [512, 512], replicated, may hold values from -0.25 to 0.25
- output_weight: bfloat16 [512, 512], replicated, may hold values from -0.25 to 0.25
Outputs:
- candidate_out: bfloat16 [512, 512], P(('parts', 'users')), parts along dimension 0
There are 2 independent parts, one for each index of `parts`. A program takes and returns all parts, laid end to end along the dimension named above; an argument that names none is the same for every part. Nothing has to cross between parts.
Inputs may be any that keep to these rules, and one draw needn't show every extreme that they name: event_user never falls along the events; each user's events form one run of at most 12288 slots.
All inputs are finite; a program needn't handle non-finite values. No bound on the sum of `event_mask` on one device may be relied on, other than what follows from the above.
Results may differ from a plain program's by a relative error of at most 0.0044.
Values may be sent and summed in bfloat16 or wider, within the bound.
No kernel may reach another device: no remote copies, remote signals or barrier semaphores. Data moves between devices by JAX's collectives and lax.ppermute only.
A program may use at most 64 MiB of HBM per device.

v0:
```python
import math
import jax
import jax.numpy as jnp
from jax import lax
from jax.sharding import PartitionSpec as P

HEADS = 4


def per_device(
    candidates,
    candidate_user,
    events,
    event_user,
    event_mask,
    query_weight,
    key_weight,
    value_weight,
    gate_weight,
    output_weight,
):
    own_count = candidates.shape[0]
    model_width = candidates.shape[1]
    head_count = HEADS
    head_size = model_width // head_count
    score_scale = 1.0 / math.sqrt(head_size)
    queries = jnp.dot(candidates, query_weight, preferred_element_type=jnp.float32).astype(
        jnp.bfloat16
    )
    gate_values = jax.nn.silu(jnp.dot(candidates, gate_weight, preferred_element_type=jnp.float32))
    key_rows = jnp.dot(events, key_weight, preferred_element_type=jnp.float32).astype(jnp.bfloat16)
    value_rows = jnp.dot(events, value_weight, preferred_element_type=jnp.float32).astype(
        jnp.bfloat16
    )
    event_count = key_rows.shape[0]
    key_heads = key_rows.reshape(event_count, head_count, head_size)
    value_heads = value_rows.reshape(event_count, head_count, head_size)
    valid_events = event_mask.astype(jnp.float32)
    all_queries, all_users = (
        lax.all_gather(queries, "users", axis=0, tiled=True),
        lax.all_gather(candidate_user, "users", axis=0, tiled=True),
    )

    def one_block(block_pair):
        query_block, user_block = block_pair
        scores = (
            jnp.einsum("chd,ehd->hce", query_block, key_heads, preferred_element_type=jnp.float32)
            * score_scale
        )
        same_user = (user_block[:, None] == event_user[None, :]).astype(jnp.float32) * valid_events[
            None, :
        ]
        attn_weights = (jax.nn.silu(scores) * same_user[None]).astype(jnp.bfloat16)
        mixed_rows = jnp.einsum(
            "hce,ehd->chd", attn_weights, value_heads, preferred_element_type=jnp.float32
        )
        return mixed_rows.reshape(query_block.shape[0], model_width)

    row_count = own_count * lax.axis_size("users")
    row_block = math.gcd(row_count, 512)
    query_part = all_queries
    query_part = query_part.reshape(row_count // row_block, row_block, head_count, head_size)
    user_part = all_users.reshape(row_count // row_block, row_block)
    summed = lax.psum_scatter(
        lax.map(one_block, (query_part, user_part)).reshape(row_count, model_width),
        "users",
        scatter_dimension=0,
        tiled=True,
    )
    mean_row = jnp.mean(summed, axis=1, keepdims=True)
    centred = summed - mean_row
    var_row = jnp.mean(centred * centred, axis=1, keepdims=True)
    normed = centred / jnp.sqrt(var_row + 1e-05)
    gated_rows = (normed * gate_values).astype(jnp.bfloat16)
    result = candidates.astype(jnp.float32) + jnp.dot(
        gated_rows, output_weight, preferred_element_type=jnp.float32
    )
    return result.astype(jnp.bfloat16)


def solution(mesh):
    in_specs = (
        P(("parts", "users"), None),
        P(("parts", "users")),
        P(("parts", "users"), None),
        P(("parts", "users")),
        P(("parts", "users")),
        P(),
        P(),
        P(),
        P(),
        P(),
    )
    out_specs = P(("parts", "users"), None)
    return jax.shard_map(
        per_device, mesh=mesh, in_specs=in_specs, out_specs=out_specs, check_vma=False
    )
```

profile of v0, /device:TPU:0, one launch (start us, length us, event | category | flops | bytes accessed | tf_op | source)
XLA Modules:
  0.0 126.6 jit_solution(15532757817765731174)
XLA Ops:
  6.5 0.0 copy-start
  6.5 0.0 reduce-scatter.2.cloned.1.call-start
  6.5 1.4 %dynamic-slice.1 = u32[1]{0:T(128)} dynamic-slice(u32[32]{0:T(128)} %constant.34, u32[]{:T(128)S(6)} %add.28), dynamic_slice_sizes={1} | dynamic-slice | bytes 12
  8.6 0.9 dynamic-update-slice
  9.4 13.7 %all-reduce = s32[256]{0:T(256)S(1)} all-reduce(s32[256]{0:T(256)S(1)} %dynamic-update-slice), channel_id=1, replica_groups=mesh['parts'=2,'users'=16] {'users'}, use_global_device_ids=true, to_apply=%add | all-reduce | flops 256 | bytes 2048
  23.2 0.7 convert_element_type.31
  23.9 1.2 convolution_convert_fusion.2
  25.1 18.7 %all_gather.6 = bf16[256,512]{1,0:T(8,128)(2,1)S(1)} all-gather(bf16[16,512]{1,0:T(8,128)(2,1)S(1)} %convolution_convert_fusion.2), channel_id=1, replica_groups=mesh['parts'=2,'users'=16] {'users'}, dimensions={0}, use_global_device_ids=true | all-gather | bytes 278528 | tf_op jit(solution)/shard_map/all_gather | solution.py:40
  43.8 0.0 copy-done
  43.8 0.0 copy-start.5
  43.8 3.7 %convolution_convert_fusion = bf16[2048,512]{0,1:T(8,128)(2,1)} fusion(bf16[2048,512]{1,0:T(8,128)(2,1)S(1)} %copy-done, bf16[512,512]{1,0:T(8,128)(2,1)} %param.16), kind=kOutput, calls=%fused_computation.1 | convolution fusion | flops 1074790400 | bytes 4718592 | tf_op jit(solution)/shard_map/dot_general | solution.py:31
  47.5 0.0 copy-done.5
  47.5 0.0 copy-start.4
  47.5 2.7 %convolution_convert_fusion.1 = bf16[2048,512]{0,1:T(8,128)(2,1)} fusion(bf16[2048,512]{1,0:T(8,128)(2,1)S(1)} %copy-done, bf16[512,512]{1,0:T(8,128)(2,1)S(1)} %copy-done.5), kind=kOutput, calls=%fused_computation.2 | convolution fusion | flops 1074790400 | bytes 4718592 | tf_op jit(solution)/shard_map/dot_general | solution.py:32
  50.1 0.0 copy-done.4
  50.1 1.5 %compare_select_fusion = f32[256,2048]{1,0:T(8,128)} fusion(f32[2048]{0:T(1024)S(1)} %convert_element_type.31, s32[2048]{0:T(1024)S(1)} %copy-done.4, s32[256]{0:T(256)S(1)} %all-reduce), kind=kLoop, calls=%fused_computation.3 | loop fusion | flops 1048576 | bytes 2114560 | tf_op jit(solution)/shard_map/while/body/eval_jaxpr/mul | solution.py:50
  51.7 0.0 copy-start.1
  51.7 0.0 copy-start.2
  51.7 0.0 copy-start.3
  51.7 8.2 %fusion = f32[4,128,256]{2,1,0:T(8,128)} fusion(bf16[2048,4,128]{0,2,1:T(8,128)(2,1)} %bitcast.28, bf16[2048,4,128]{0,2,1:T(8,128)(2,1)} %bitcast.27, f32[256,2048]{1,0:T(8,128)} %compare_select_fusion, bf16[256,512]{1,0:T(8,128)(2,1)S(1)} %all_gather.6), kind=kOutput, calls=%fused_computation.4 | convolution fusion | flops 1088421888 | bytes 7077888 | tf_op jit(solution)/shard_map/while/body/eval_jaxpr/hce,ehd->chd/dot_general | solution.py:54
  59.9 2.0 %copy.13 = f32[256,512]{1,0:T(8,128)} copy(f32[256,512]{0,1:T(8,128)} %bitcast.26) | data formatting | bytes 1048576 | tf_op jit(solution)/shard_map/reshape | solution.py:65
  61.9 0.0 reduce-scatter.2.cloned.1.call-update
  61.9 54.3 %reduce-scatter.2.cloned.1.call-done = f32[16,512]{1,0:T(8,128)} async-done(((f32[256,512]{1,0:T(8,128)}), f32[16,512]{1,0:T(8,128)}) %reduce-scatter.2.cloned.1.call-update) | async-done | bytes 32784 | tf_op jit(solution)/shard_map/reduce_scatter | solution.py:64
  116.2 0.9 reduce_sum.18
  117.1 0.9 multiply_reduce_fusion
  118.0 0.0 copy-done.1
  118.0 0.0 copy-done.2
  118.1 0.0 copy-done.3
  118.1 1.7 %fusion.1 = bf16[16,512]{1,0:T(8,128)(2,1)} fusion(bf16[512,512]{1,0:T(8,128)(2,1)S(1)} %copy-done.1, bf16[16,512]{1,0:T(8,128)(2,1)S(1)} %copy-done.3, f32[16,512]{1,0:T(8,128)} %reduce-scatter.2.cloned.1.call-done, f32[16]{0:T(128)S(1)} %add_sqrt_fusion, f32[16]{0:T(128)S(1)} %broadcast_multiply_fusion, bf16[512,512]{1,0:T(8,128)(2,1)S(1)} %copy-done.2), kind=kOutput, calls=%fused_computation.6 | convolution fusion | flops 16867328 | bytes 1114240 | tf_op jit(solution)/shard_map/dot_general | solution.py:75
  (3 shorter events, 0.0 us)
Async XLA Ops:
  6.5 37.2 %copy-start = (bf16[2048,512]{1,0:T(8,128)(2,1)S(1)}, bf16[2048,512]{1,0:T(8,128)(2,1)}, u32[]{:S(2)}) copy-start(bf16[2048,512]{1,0:T(8,128)(2,1)} %param.12) | copy-start | bytes 6291460
  6.5 109.7 %reduce-scatter.2.cloned.1.call-start = ((), (), s32[]{:S(2)}) async-start(), calls=%async_computation.1 | async-start | bytes 557056 | tf_op jit(solution)/shard_map/reduce_scatter | solution.py:64
  43.8 3.7 %copy-start.5 = (bf16[512,512]{1,0:T(8,128)(2,1)S(1)}, bf16[512,512]{1,0:T(8,128)(2,1)}, u32[]{:S(2)}) copy-start(bf16[512,512]{1,0:T(8,128)(2,1)} %param.17) | copy-start | bytes 1572868
  47.5 2.7 %copy-start.4 = (s32[2048]{0:T(1024)S(1)}, s32[2048]{0:T(1024)}, u32[]{:S(2)}) copy-start(s32[2048]{0:T(1024)} %param.13) | copy-start | bytes 24580
  51.7 66.4 %copy-start.1 = (bf16[512,512]{1,0:T(8,128)(2,1)S(1)}, bf16[512,512]{1,0:T(8,128)(2,1)}, u32[]{:S(2)}) copy-start(bf16[512,512]{1,0:T(8,128)(2,1)} %param.19) | copy-start | bytes 1572868
  51.7 66.4 %copy-start.2 = (bf16[512,512]{1,0:T(8,128)(2,1)S(1)}, bf16[512,512]{1,0:T(8,128)(2,1)}, u32[]{:S(2)}) copy-start(bf16[512,512]{1,0:T(8,128)(2,1)} %param.18) | copy-start | bytes 1572868
  51.7 66.4 %copy-start.3 = (bf16[16,512]{1,0:T(8,128)(2,1)S(1)}, bf16[16,512]{1,0:T(8,128)(2,1)}, u32[]{:S(2)}) copy-start(bf16[16,512]{1,0:T(8,128)(2,1)} %param.10) | copy-start | bytes 49156
Sparse Core Ops, SparseCore 0:
  62.0 54.1 reduce-scatter.1
where the time goes:
time: 127 us
  waiting for transfers between devices  54.3 us (43%)
  blocking collectives  32.4 us (26%)
  matrix products  17.5 us (14%)
  between operations  14.1 us (11%)
  local copies, waits for them, and re-layouts  4.3 us (3%)
  other arithmetic  4.07 us (3%)
    reduce_scatter x1, waiting for transfers between devices, per_device(): lax.psum_scatter(lax.map(one_block, (query_part, user_part)).reshape(row_...  54.3 us
    all_gather x1, blocking collectives, per_device(): lax.all_gather(queries, 'users', axis=0, tiled=True)  18.7 us
    unnamed x1, blocking collectives  13.7 us
    dot_general x1, matrix products, one_block(): jnp.einsum('hce,ehd->chd', attn_weights, value_heads, preferred_element_t...  8.19 us
    dot_general x1, matrix products, per_device(): jnp.dot(events, key_weight, preferred_element_type=jnp.float32)  3.69 us
    dot_general x1, matrix products, per_device(): jnp.dot(events, value_weight, preferred_element_type=jnp.float32)  2.65 us
  transfers between devices with their start and end apart: 1, of which 1 were waited for; matrix products, arithmetic and copies ran while one was open for 0% of the time, Pallas kernels for 0%

commit v1 on v0

--- a/solution.py
+++ b/solution.py
@@ -37,7 +37,9 @@
     value_heads = value_rows.reshape(event_count, head_count, head_size)
     valid_events = event_mask.astype(jnp.float32)
     all_queries, all_users = (
-        lax.all_gather(queries, "users", axis=0, tiled=True),
+        jnp.concatenate(
+            lax.all_to_all(jnp.stack([queries] * lax.axis_size("users")), "users", 0, 0), axis=0
+        ),
         lax.all_gather(candidate_user, "users", axis=0, tiled=True),
     )
 

time: 127 us -> 115 us (0.906)
  blocking collectives: 32.4 us -> 12.4 us
  starting transfers between devices: 0.01 us -> 7.43 us
    all_gather x1 -> x0, blocking collectives: 18.7 us -> none  [per_device(): lax.all_gather(queries, 'users', axis=0, tiled=True)]
    all_to_all x0 -> x1, starting transfers between devices: none -> 7.39 us  [per_device(): lax.all_to_all(jnp.stack([queries] * lax.axis_size('users')), 'users', 0, 0)]
    unnamed x1, blocking collectives: 13.7 us -> 12.4 us
  transfers between devices with their start and end apart: 1 -> 2, of which waited for: 1 -> 1; matrix products, arithmetic and copies ran while one was open for 0% -> 9% of each run, Pallas kernels for 0% -> 0%
where the time goes in v1:
time: 115 us
  waiting for transfers between devices  53.9 us (47%)
  matrix products  17.7 us (15%)
  between operations  14.1 us (12%)
  blocking collectives  12.4 us (11%)
  starting transfers between devices  7.43 us (6%)
  local copies, waits for them, and re-layouts  4.98 us (4%)
  other arithmetic  4.07 us (4%)
    reduce_scatter x1, waiting for transfers between devices, per_device(): lax.psum_scatter(lax.map(one_block, (query_part, user_part)).reshape(row_...  53.9 us
    unnamed x1, blocking collectives  12.4 us
    dot_general x1, matrix products, one_block(): jnp.einsum('hce,ehd->chd', attn_weights, value_heads, preferred_element_t...  8.25 us
    all_to_all x1, starting transfers between devices, per_device(): lax.all_to_all(jnp.stack([queries] * lax.axis_size('users')), 'users', 0, 0)  7.39 us
    dot_general x1, matrix products, per_device(): jnp.dot(events, key_weight, preferred_element_type=jnp.float32)  3.69 us
    dot_general x1, matrix products, per_device(): jnp.dot(events, value_weight, preferred_element_type=jnp.float32)  2.65 us
  transfers between devices with their start and end apart: 2, of which 1 were waited for; matrix products, arithmetic and copies ran while one was open for 9% of the time, Pallas kernels for 0%

profile of v1, /device:TPU:0, one launch (start us, length us, event | category | flops | bytes accessed | tf_op | source)
XLA Modules:
  0.0 114.6 jit_solution(9066931620304522641)
XLA Ops:
  6.5 0.0 copy-start
  6.5 1.4 %convolution_convert_fusion.2 = bf16[16,512]{1,0:T(8,128)(2,1)S(1)} fusion(bf16[16,512]{1,0:T(8,128)(2,1)} %param.10, bf16[512,512]{1,0:T(8,128)(2,1)} %param.15), kind=kOutput, calls=%fused_computation.7 | convolution fusion | flops 8396800 | bytes 557056 | tf_op jit(solution)/shard_map/dot_general | solution.py:27
  7.9 0.8 stack.2
  8.7 7.4 %all-to-all-start = ((bf16[16,16,512]{2,1,0:T(8,128)(2,1)}), bf16[16,16,512]{2,1,0:T(8,128)(2,1)S(1)}, u32[]{:S(2)}, u32[]{:S(2)}) async-start(bf16[16,16,512]{2,1,0:T(8,128)(2,1)} %stack.2), calls=%async_computation | async-start | bytes 524288 | tf_op jit(solution)/shard_map/all_to_all | solution.py:41
  16.1 0.0 reduce-scatter.2.cloned.1.call-start
  16.1 1.2 %dynamic-slice.1 = u32[1]{0:T(128)} dynamic-slice(u32[32]{0:T(128)} %constant.34, u32[]{:T(128)S(6)} %add.28), dynamic_slice_sizes={1} | dynamic-slice | bytes 12
  18.0 0.9 dynamic-update-slice
  18.9 12.4 %all-reduce = s32[256]{0:T(256)S(1)} all-reduce(s32[256]{0:T(256)S(1)} %dynamic-update-slice), channel_id=1, replica_groups=mesh['parts'=2,'users'=16] {'users'}, use_global_device_ids=true, to_apply=%add | all-reduce | flops 256 | bytes 2048
  31.3 0.7 convert_element_type.31
  32.0 0.0 copy-done
  32.0 0.0 copy-start.5
  32.0 3.7 %convolution_convert_fusion = bf16[2048,512]{0,1:T(8,128)(2,1)} fusion(bf16[2048,512]{1,0:T(8,128)(2,1)S(1)} %copy-done, bf16[512,512]{1,0:T(8,128)(2,1)} %param.16), kind=kOutput, calls=%fused_computation.1 | convolution fusion | flops 1074790400 | bytes 4718592 | tf_op jit(solution)/shard_map/dot_general | solution.py:31
  35.7 0.0 copy-done.5
  35.7 0.0 copy-start.4
  35.7 2.7 %convolution_convert_fusion.1 = bf16[2048,512]{0,1:T(8,128)(2,1)} fusion(bf16[2048,512]{1,0:T(8,128)(2,1)S(1)} %copy-done, bf16[512,512]{1,0:T(8,128)(2,1)S(1)} %copy-done.5), kind=kOutput, calls=%fused_computation.2 | convolution fusion | flops 1074790400 | bytes 4718592 | tf_op jit(solution)/shard_map/dot_general | solution.py:32
  38.4 0.0 copy-done.4
  38.4 1.5 %compare_select_fusion = f32[256,2048]{1,0:T(8,128)} fusion(f32[2048]{0:T(1024)S(1)} %convert_element_type.31, s32[2048]{0:T(1024)S(1)} %copy-done.4, s32[256]{0:T(256)S(1)} %all-reduce), kind=kLoop, calls=%fused_computation.3 | loop fusion | flops 1048576 | bytes 2114560 | tf_op jit(solution)/shard_map/while/body/eval_jaxpr/mul | solution.py:52
  39.9 0.0 all-to-all-done
  39.9 0.1 squeeze.8
  40.0 0.0 copy-start.1
  40.0 0.0 copy-start.2
  40.0 0.0 copy-start.3
  40.0 8.2 %fusion = f32[4,128,256]{2,1,0:T(8,128)} fusion(bf16[2048,4,128]{0,2,1:T(8,128)(2,1)} %bitcast.19, bf16[2048,4,128]{0,2,1:T(8,128)(2,1)} %bitcast.18, f32[256,2048]{1,0:T(8,128)} %compare_select_fusion, bf16[256,4,128]{2,1,0:T(4,128)(2,1)S(1)} %squeeze.8), kind=kOutput, calls=%fused_computation.4 | convolution fusion | flops 1088421888 | bytes 7077888 | tf_op jit(solution)/shard_map/while/body/eval_jaxpr/hce,ehd->chd/dot_general | solution.py:56
  48.3 2.0 %copy.15 = f32[256,512]{1,0:T(8,128)} copy(f32[256,512]{0,1:T(8,128)} %bitcast.17) | data formatting | bytes 1048576 | tf_op jit(solution)/shard_map/reshape | solution.py:67
  50.3 0.0 reduce-scatter.2.cloned.1.call-update
  50.3 53.9 %reduce-scatter.2.cloned.1.call-done = f32[16,512]{1,0:T(8,128)} async-done(((f32[256,512]{1,0:T(8,128)}), f32[16,512]{1,0:T(8,128)}) %reduce-scatter.2.cloned.1.call-update) | async-done | bytes 32784 | tf_op jit(solution)/shard_map/reduce_scatter | solution.py:66
  104.2 0.9 reduce_sum.18
  105.1 0.9 multiply_reduce_fusion
  106.0 0.0 copy-done.1
  106.0 0.0 copy-done.2
  106.0 0.0 copy-done.3
  106.0 1.7 %fusion.1 = bf16[16,512]{1,0:T(8,128)(2,1)} fusion(bf16[512,512]{1,0:T(8,128)(2,1)S(1)} %copy-done.1, bf16[16,512]{1,0:T(8,128)(2,1)S(1)} %copy-done.3, f32[16,512]{1,0:T(8,128)} %reduce-scatter.2.cloned.1.call-done, f32[16]{0:T(128)S(1)} %add_sqrt_fusion, f32[16]{0:T(128)S(1)} %broadcast_multiply_fusion, bf16[512,512]{1,0:T(8,128)(2,1)S(1)} %copy-done.2), kind=kOutput, calls=%fused_computation.6 | convolution fusion | flops 16867328 | bytes 1114240 | tf_op jit(solution)/shard_map/dot_general | solution.py:77
  (3 shorter events, 0.0 us)
Async XLA Ops:
  6.5 25.5 %copy-start = (bf16[2048,512]{1,0:T(8,128)(2,1)S(1)}, bf16[2048,512]{1,0:T(8,128)(2,1)}, u32[]{:S(2)}) copy-start(bf16[2048,512]{1,0:T(8,128)(2,1)} %param.12) | copy-start | bytes 6291460
  8.7 31.2 %all-to-all-start = ((bf16[16,16,512]{2,1,0:T(8,128)(2,1)}), bf16[16,16,512]{2,1,0:T(8,128)(2,1)S(1)}, u32[]{:S(2)}, u32[]{:S(2)}) async-start(bf16[16,16,512]{2,1,0:T(8,128)(2,1)} %stack.2), calls=%async_computation | async-start | bytes 524288 | tf_op jit(solution)/shard_map/all_to_all | solution.py:41
  16.1 88.1 %reduce-scatter.2.cloned.1.call-start = ((), (), s32[]{:S(2)}) async-start(), calls=%async_computation.2 | async-start | bytes 557056 | tf_op jit(solution)/shard_map/reduce_scatter | solution.py:66
  32.0 3.7 %copy-start.5 = (bf16[512,512]{1,0:T(8,128)(2,1)S(1)}, bf16[512,512]{1,0:T(8,128)(2,1)}, u32[]{:S(2)}) copy-start(bf16[512,512]{1,0:T(8,128)(2,1)} %param.17) | copy-start | bytes 1572868
  35.7 2.7 %copy-start.4 = (s32[2048]{0:T(1024)S(1)}, s32[2048]{0:T(1024)}, u32[]{:S(2)}) copy-start(s32[2048]{0:T(1024)} %param.13) | copy-start | bytes 24580
  40.0 66.0 %copy-start.1 = (bf16[512,512]{1,0:T(8,128)(2,1)S(1)}, bf16[512,512]{1,0:T(8,128)(2,1)}, u32[]{:S(2)}) copy-start(bf16[512,512]{1,0:T(8,128)(2,1)} %param.19) | copy-start | bytes 1572868
  40.0 66.0 %copy-start.2 = (bf16[512,512]{1,0:T(8,128)(2,1)S(1)}, bf16[512,512]{1,0:T(8,128)(2,1)}, u32[]{:S(2)}) copy-start(bf16[512,512]{1,0:T(8,128)(2,1)} %param.18) | copy-start | bytes 1572868
  40.0 66.0 %copy-start.3 = (bf16[16,512]{1,0:T(8,128)(2,1)S(1)}, bf16[16,512]{1,0:T(8,128)(2,1)}, u32[]{:S(2)}) copy-start(bf16[16,512]{1,0:T(8,128)(2,1)} %param.10) | copy-start | bytes 49156
Sparse Core Ops, SparseCore 0:
  50.4 53.7 reduce-scatter.1
